TPU v7x, 32 devices: a whole 2x2x4 slice. The times are simulated.
32 devices in a mesh: row: 2 (over y), pair: 16 (over z, x, core).
Axes of the slice: x: 2, y: 2, z: 4, core: 2. Of those that a mesh axis runs over, the one named last changes fastest.
Arguments:
- panel: float32 [4096, 4096], P('row', 'pair'), may hold values from -51 to 51
- slot_block: int32 [32], replicated, may hold values from 0 to 31, each once
Outputs:
- rotated: float32 [4096, 4096], P('row', 'pair')
Inputs may be any that keep to these rules, and one draw needn't show every extreme that they name: `slot_block`: each block number appears once.
All inputs are finite; a program needn't handle non-finite values.
Results may differ from a plain program's by a relative error of at most 0.0003.
Values sent between devices are 32-bit elements; how exact they have to be, the bound alone decides.
A program may use at most 64 MiB of HBM per device.

v0:
```python
import jax
import jax.numpy as jnp
from jax import lax
from jax.sharding import PartitionSpec as P

STEPS = 2
NS_ITERS = 3
precise = lax.Precision.HIGHEST


def passed_along(value, axis, steps):
    count = lax.axis_size(axis)
    initial, last = (max(0, -steps), min(count, count - steps))
    return lax.ppermute(value, axis, [(source, source + steps) for source in range(initial, last)])


def inverse_root(matrix):
    identity = jnp.eye(matrix.shape[0], dtype=matrix.dtype)
    approx = matrix
    root_inv = identity
    for sweep in range(NS_ITERS):
        factor = 1.5 * identity - 0.5 * jnp.dot(root_inv, approx, precision=precise)
        approx = jnp.dot(approx, factor, precision=precise)
        root_inv = jnp.dot(factor, root_inv, precision=precise)
    return root_inv / jnp.sqrt(5.0)


def couple(cross):
    identity = jnp.eye(cross.shape[0], dtype=cross.dtype)
    coupling = cross * (2.0 / jnp.sqrt(jnp.sum(cross * cross) + 1e-06))
    left = (identity + jnp.dot(coupling, coupling.T, precision=precise)) / 5.0
    right = (identity + jnp.dot(coupling.T, coupling, precision=precise)) / 5.0
    return (coupling, left, right)


def inner_rows(first, second):
    return lax.dot_general(first, second, (((0,), (0,)), ((), ())), precision=precise)


def move_slots(uppers, lowers):
    new_uppers = jnp.concatenate([uppers[0:1], lowers[0:1], uppers[1:-1]], axis=0)
    new_lowers = jnp.concatenate([lowers[1:], uppers[-1:]], axis=0)
    return (new_uppers, new_lowers)


def jacobi_step(upper, lower, upper_ids, lower_ids, position, pairs):
    matching = jnp.arange(pairs) == position
    upper_id = jnp.sum(jnp.where(matching, upper_ids, 0))
    lower_id = jnp.sum(jnp.where(matching, lower_ids, 0))
    order_flag = upper_id < lower_id
    first = jnp.where(order_flag, upper, lower)
    second = jnp.where(order_flag, lower, upper)
    cross = lax.psum(inner_rows(first, second), "row")
    coupling, left, right = couple(cross)
    left_inverse = inverse_root(left)
    right_inverse = inverse_root(right)
    new_first = jnp.dot(
        first + jnp.dot(second, coupling.T, precision=precise), left_inverse, precision=precise
    )
    new_second = jnp.dot(
        second - jnp.dot(first, coupling, precision=precise), right_inverse, precision=precise
    )
    new_upper = jnp.where(order_flag, new_first, new_second)
    new_lower = jnp.where(order_flag, new_second, new_first)
    carried = jnp.where(position == 0, new_lower, new_upper)
    from_left = passed_along(carried, "pair", 1)
    from_right = passed_along(new_lower, "pair", -1)
    moved_upper = jnp.where(position == 0, new_upper, from_left)
    moved_lower = jnp.where(position == pairs - 1, new_upper, from_right)
    return (moved_upper, moved_lower)


def per_device(panel, slot_block):
    width = panel.shape[1] // 2
    pairs = lax.axis_size("pair")
    position = lax.axis_index("pair")
    upper = panel[:, :width]
    lower = panel[:, width:]
    upper_ids = slot_block[:pairs]
    lower_ids = slot_block[pairs:]
    for step in range(STEPS):
        upper, lower = jacobi_step(upper, lower, upper_ids, lower_ids, position, pairs)
        upper_ids, lower_ids = move_slots(upper_ids, lower_ids)
    return jnp.concatenate([upper, lower], axis=1)


def solution(mesh):
    in_specs = (P("row", "pair"), P())
    out_specs = P("row", "pair")
    return jax.shard_map(
        per_device, mesh=mesh, in_specs=in_specs, out_specs=out_specs, check_vma=False
    )
```

profile of v0, /device:TPU:9, one launch (start us, length us, event | category | flops | bytes accessed | tf_op | source)
XLA Modules:
  0.0 150.3 jit_solution(13770389145376605013)
XLA Ops:
  6.5 1.5 %select_reduce_fusion = (s32[]{:T(128)}, s32[]{:T(128)}) fusion(s32[32]{0:T(128)} %param.3, s32[]{:T(128)S(6)} %axis_index.12), kind=kLoop, calls=%fused_computation.82 | loop fusion | flops 78 | bytes 140 | tf_op jit(solution)/shard_map/reduce_sum | solution.py:49
  9.4 1.7 %slice_select_fusion.1 = (f32[2048,128]{1,0:T(8,128)S(1)}, f32[2048,128]{1,0:T(8,128)S(1)}) fusion(f32[2048,256]{1,0:T(8,128)} %param.2, pred[]{:T(512)S(6)} %lt.7), kind=kLoop, calls=%fused_computation.42 | loop fusion | flops 524288 | bytes 4194305 | tf_op jit(solution)/shard_map/jit(_where)/select_n | solution.py:51
  11.1 2.4 %fusion.39 = f32[128,128]{1,0:T(8,128)} fusion(f32[2048,128]{1,0:T(8,128)S(1)} %get-tuple-element.15, f32[2048,128]{1,0:T(8,128)S(1)} %get-tuple-element.16), kind=kOutput, calls=%fused_computation.86 | convolution fusion | flops 402653184 | bytes 2162688 | tf_op jit(solution)/shard_map/dot_general | solution.py:37
  13.6 21.8 %all-reduce.3.cloned.1.call-done = f32[128,128]{1,0:T(8,128)} async-done(((f32[128,128]{1,0:T(8,128)}), f32[128,128]{1,0:T(8,128)}) %all-reduce.3.cloned.1.call-update) | async-done | bytes 65552 | tf_op jit(solution)/shard_map/psum | solution.py:53
  35.4 1.5 %multiply_reduce_fusion.1 = f32[]{:T(128)} fusion(f32[128,128]{1,0:T(8,128)} %all-reduce.3.cloned.1.call-done), kind=kLoop, calls=%fused_computation.61 | loop fusion | flops 32767 | bytes 65540 | tf_op jit(solution)/shard_map/reduce_sum | solution.py:30
  37.6 1.2 fusion.11
  40.0 1.2 fusion.15
  43.3 1.0 convolution_add_fusion.1
  44.3 1.0 fusion.43
  45.3 1.0 convolution_subtract_fusion.1
  46.3 2.0 %broadcast_select_fusion.11 = (f32[2048,128]{1,0:T(8,128)}, f32[2048,128]{1,0:T(8,128)S(1)}, f32[2048,128]{1,0:T(8,128)S(1)}) fusion(pred[]{:T(512)S(6)} %eq.72, f32[2048,128]{1,0:T(8,128)S(1)} %fusion.43, pred[]{:T(512)S(6)} %lt.7, f32[2048,128]{1,0:T(8,128)S(1)} %convolution_subtract_fusion.1, f32[128,128]{1,0:T(8,128)S(1)} %convolution_multiply_fusion.8), kind=kOutput, calls=%fused_computation.54 | convolution fusion | flops 403439616 | bytes 5308418 | tf_op jit(solution)/shard_map/dot_general | solution.py:60
  48.3 4.1 %collective-permute-start = (f32[2048,128]{1,0:T(8,128)}, f32[2048,128]{1,0:T(8,128)S(1)}, u32[]{:S(2)}, u32[]{:S(2)}) collective-permute-start(f32[2048,128]{1,0:T(8,128)} %get-tuple-element.10), channel_id=1, source_target_pairs={{0,1},{1,2},{2,3},{3,4},{4,5},{5,6},{6,7},{7,8},{8,9},{9,10},{10,1... | collective-permute-start | bytes 3145736 | tf_op jit(solution)/shard_map/ppermute | solution.py:14
  52.4 2.1 %collective-permute-start.1 = (f32[2048,128]{1,0:T(8,128)S(1)}, f32[2048,128]{1,0:T(8,128)}, u32[]{:S(2)}, u32[]{:S(2)}) collective-permute-start(f32[2048,128]{1,0:T(8,128)S(1)} %get-tuple-element.11), channel_id=1, source_target_pairs={{1,0},{2,1},{3,2},{4,3},{5,4},{6,5},{7,6},{8,7},{9,8},{10,9},{11,1... | collective-permute-start | bytes 3145736 | tf_op jit(solution)/shard_map/ppermute | solution.py:14
  54.6 0.7 fusion.38
  55.3 2.6 %fusion.36 = (s32[]{:T(128)}, s32[]{:T(128)}) fusion(s32[14]{0:T(128)S(1)} %slice.34, s32[1]{0:T(128)} %get-tuple-element.20, s32[1]{0:T(128)} %get-tuple-element.21, s32[]{:T(128)S(6)} %axis_index.12, s32[1]{0:T(128)} %get-tuple-element.19, s32[15]{0:T(128)S(1)} %slice.35), kind=kLoop, calls=%fused_computation.79 | loop fusion | flops 126 | bytes 140 | tf_op jit(solution)/shard_map/reduce_sum | solution.py:48
  59.2 16.5 %collective-permute-done = f32[2048,128]{1,0:T(8,128)S(1)} collective-permute-done((f32[2048,128]{1,0:T(8,128)}, f32[2048,128]{1,0:T(8,128)S(1)}, u32[]{:S(2)}, u32[]{:S(2)}) %collective-permute-start) | collective-permute-done | bytes 1048608 | tf_op jit(solution)/shard_map/ppermute | solution.py:14
  75.7 1.6 %collective-permute-done.1 = f32[2048,128]{1,0:T(8,128)} collective-permute-done((f32[2048,128]{1,0:T(8,128)S(1)}, f32[2048,128]{1,0:T(8,128)}, u32[]{:S(2)}, u32[]{:S(2)}) %collective-permute-start.1) | collective-permute-done | bytes 1048608 | tf_op jit(solution)/shard_map/ppermute | solution.py:14
  77.3 1.7 %broadcast_select_fusion.7 = (f32[2048,128]{1,0:T(8,128)S(1)}, f32[2048,128]{1,0:T(8,128)S(1)}) fusion(pred[]{:T(512)S(6)} %lt.6, f32[2048,128]{1,0:T(8,128)S(1)} %get-tuple-element.12, f32[2048,128]{1,0:T(8,128)} %copy-done.2, pred[]{:T(512)S(6)} %eq.72, f32[2048,128]{1,0:T(8,128)} %collective-permute-done.1, pred[]{:T(512)S(6)} %eq.76), kind=kLoop, calls=%fused_computation.50 | loop fusion | flops 1048576 | bytes 5242883 | tf_op jit(solution)/shard_map/jit(_where)/select_n | solution.py:51
  79.0 2.4 %fusion.47 = f32[128,128]{1,0:T(8,128)} fusion(f32[2048,128]{1,0:T(8,128)S(1)} %get-tuple-element.13, f32[2048,128]{1,0:T(8,128)S(1)} %get-tuple-element.14), kind=kOutput, calls=%fused_computation.94 | convolution fusion | flops 402653184 | bytes 2162688 | tf_op jit(solution)/shard_map/dot_general | solution.py:37
  81.5 19.7 %all-reduce.5.cloned.1.call-done = f32[128,128]{1,0:T(8,128)} async-done(((f32[128,128]{1,0:T(8,128)}), f32[128,128]{1,0:T(8,128)}) %all-reduce.5.cloned.1.call-update) | async-done | bytes 65552 | tf_op jit(solution)/shard_map/psum | solution.py:53
  101.2 1.5 %multiply_reduce_fusion = f32[]{:T(128)} fusion(f32[128,128]{1,0:T(8,128)} %all-reduce.5.cloned.1.call-done), kind=kLoop, calls=%fused_computation.55 | loop fusion | flops 32767 | bytes 65540 | tf_op jit(solution)/shard_map/reduce_sum | solution.py:30
  103.4 1.2 fusion.3
  105.8 1.2 fusion.7
  109.1 1.0 convolution_add_fusion
  110.1 1.0 fusion.51
  111.1 1.0 convolution_subtract_fusion
  112.1 1.0 broadcast_select_fusion.9
  113.1 4.1 %collective-permute-start.2 = (f32[2048,128]{1,0:T(8,128)S(1)}, f32[2048,128]{1,0:T(8,128)S(1)}, u32[]{:S(2)}, u32[]{:S(2)}) collective-permute-start(f32[2048,128]{1,0:T(8,128)S(1)} %get-tuple-element.7), channel_id=1, source_target_pairs={{0,1},{1,2},{2,3},{3,4},{4,5},{5,6},{6,7},{7,8},{8,9},{9,10},{10,1... | collective-permute-start | bytes 3145736 | tf_op jit(solution)/shard_map/ppermute | solution.py:14
  117.2 1.9 %collective-permute-start.3 = (f32[2048,128]{1,0:T(8,128)S(1)}, f32[2048,128]{1,0:T(8,128)S(1)}, u32[]{:S(2)}, u32[]{:S(2)}) collective-permute-start(f32[2048,128]{1,0:T(8,128)S(1)} %get-tuple-element.8), channel_id=1, source_target_pairs={{1,0},{2,1},{3,2},{4,3},{5,4},{6,5},{7,6},{8,7},{9,8},{10,9},{11,1... | collective-permute-start | bytes 3145736 | tf_op jit(solution)/shard_map/ppermute | solution.py:14
  119.1 21.0 %collective-permute-done.2 = f32[2048,128]{1,0:T(8,128)S(1)} collective-permute-done((f32[2048,128]{1,0:T(8,128)S(1)}, f32[2048,128]{1,0:T(8,128)S(1)}, u32[]{:S(2)}, u32[]{:S(2)}) %collective-permute-start.2) | collective-permute-done | bytes 1048608 | tf_op jit(solution)/shard_map/ppermute | solution.py:14
  140.2 1.6 %collective-permute-done.3 = f32[2048,128]{1,0:T(8,128)S(1)} collective-permute-done((f32[2048,128]{1,0:T(8,128)S(1)}, f32[2048,128]{1,0:T(8,128)S(1)}, u32[]{:S(2)}, u32[]{:S(2)}) %collective-permute-start.3) | collective-permute-done | bytes 1048608 | tf_op jit(solution)/shard_map/ppermute | solution.py:14
  142.0 1.5 pad_maximum_fusion
  (47 shorter events, 6.8 us)
Async XLA Ops:
  6.5 28.8 %all-reduce.3.cloned.1.call-start = ((), (), s32[]{:S(2)}) async-start(), calls=%async_computation | async-start | bytes 131072 | tf_op jit(solution)/shard_map/psum | solution.py:53
  13.6 87.6 %all-reduce.5.cloned.1.call-start = ((), (), s32[]{:S(2)}) async-start(), calls=%async_computation.1 | async-start | bytes 131072 | tf_op jit(solution)/shard_map/psum | solution.py:53
  35.4 7.9 %copy-start = (f32[128,128]{1,0:T(8,128)S(1)}, f32[128,128]{1,0:T(8,128)}, u32[]{:S(2)}) copy-start(f32[128,128]{1,0:T(8,128)} %all-reduce.3.cloned.1.call-done) | copy-start | bytes 196612
  46.3 8.2 %copy-start.3 = (s32[32]{0:T(128)S(1)}, s32[32]{0:T(128)}, u32[]{:S(2)}) copy-start(s32[32]{0:T(128)} %param.3) | copy-start | bytes 388
  48.3 27.4 %collective-permute-start = (f32[2048,128]{1,0:T(8,128)}, f32[2048,128]{1,0:T(8,128)S(1)}, u32[]{:S(2)}, u32[]{:S(2)}) collective-permute-start(f32[2048,128]{1,0:T(8,128)} %get-tuple-element.10), channel_id=1, source_target_pairs={{0,1},{1,2},{2,3},{3,4},{4,5},{5,6},{6,7},{7,8},{8,9},{9,10},{10,1... | collective-permute-start | bytes 3145736 | tf_op jit(solution)/shard_map/ppermute | solution.py:14
  52.4 24.9 %collective-permute-start.1 = (f32[2048,128]{1,0:T(8,128)S(1)}, f32[2048,128]{1,0:T(8,128)}, u32[]{:S(2)}, u32[]{:S(2)}) collective-permute-start(f32[2048,128]{1,0:T(8,128)S(1)} %get-tuple-element.11), channel_id=1, source_target_pairs={{1,0},{2,1},{3,2},{4,3},{5,4},{6,5},{7,6},{8,7},{9,8},{10,9},{11,1... | collective-permute-start | bytes 3145736 | tf_op jit(solution)/shard_map/ppermute | solution.py:14
  75.7 1.6 %copy-start.2 = (f32[2048,128]{1,0:T(8,128)}, f32[2048,128]{1,0:T(8,128)S(1)}, u32[]{:S(2)}) copy-start(f32[2048,128]{1,0:T(8,128)S(1)} %collective-permute-done) | copy-start | bytes 3145732
  101.2 7.9 %copy-start.1 = (f32[128,128]{1,0:T(8,128)S(1)}, f32[128,128]{1,0:T(8,128)}, u32[]{:S(2)}) copy-start(f32[128,128]{1,0:T(8,128)} %all-reduce.5.cloned.1.call-done) | copy-start | bytes 196612
  113.1 27.1 %collective-permute-start.2 = (f32[2048,128]{1,0:T(8,128)S(1)}, f32[2048,128]{1,0:T(8,128)S(1)}, u32[]{:S(2)}, u32[]{:S(2)}) collective-permute-start(f32[2048,128]{1,0:T(8,128)S(1)} %get-tuple-element.7), channel_id=1, source_target_pairs={{0,1},{1,2},{2,3},{3,4},{4,5},{5,6},{6,7},{7,8},{8,9},{9,10},{10,1... | collective-permute-start | bytes 3145736 | tf_op jit(solution)/shard_map/ppermute | solution.py:14
  117.2 24.6 %collective-permute-start.3 = (f32[2048,128]{1,0:T(8,128)S(1)}, f32[2048,128]{1,0:T(8,128)S(1)}, u32[]{:S(2)}, u32[]{:S(2)}) collective-permute-start(f32[2048,128]{1,0:T(8,128)S(1)} %get-tuple-element.8), channel_id=1, source_target_pairs={{1,0},{2,1},{3,2},{4,3},{5,4},{6,5},{7,6},{8,7},{9,8},{10,9},{11,1... | collective-permute-start | bytes 3145736 | tf_op jit(solution)/shard_map/ppermute | solution.py:14
Sparse Core Ops, SparseCore 0:
  13.7 21.6 all-reduce.2
  81.6 19.5 all-reduce.4
where the time goes:
time: 151 us; the launch traced here: 150 us
  waiting for transfers between devices  82.3 us (55%)
  matrix products  24.9 us (16%)
  between operations  17.7 us (12%)
  starting transfers between devices  12.3 us (8%)
  other arithmetic  12.3 us (8%)
    psum x2, waiting for transfers between devices, jacobi_step(): cross = lax.psum(inner_rows(first, second), 'row')  41.5 us
    ppermute x4, waiting for transfers between devices, passed_along(): lax.ppermute(value, axis, [(source, source + steps) for source in range(i...  40.7 us
    ppermute x4, starting transfers between devices, passed_along(): lax.ppermute(value, axis, [(source, source + steps) for source in range(i...  12.2 us
    dot_general x2, matrix products, inner_rows(): lax.dot_general(first, second, (((0,), (0,)), ((), ())), precision=precise)  4.89 us
    select_n x2, other arithmetic, jacobi_step(): first = jnp.where(order_flag, upper, lower)  3.41 us
    reduce_sum x2, other arithmetic, couple(): coupling = cross * (2.0 / jnp.sqrt(jnp.sum(cross * cross) + 1e-06))  3.06 us
  transfers between devices with their start and end apart: 6, of which 6 were waited for; matrix products, arithmetic and copies ran while one was open for 2% of the time, Pallas kernels for 0%

commit v1 on v0

--- a/solution.py
+++ b/solution.py
@@ -50,7 +50,7 @@
     order_flag = upper_id < lower_id
     first = jnp.where(order_flag, upper, lower)
     second = jnp.where(order_flag, lower, upper)
-    cross = lax.psum(inner_rows(first, second), "row")
+    cross = jnp.sum(lax.all_gather(inner_rows(first, second), "row"), axis=0)
     coupling, left, right = couple(cross)
     left_inverse = inverse_root(left)
     right_inverse = inverse_root(right)

time: 151 us -> 99.5 us (0.66)
  waiting for transfers between devices: 82.3 us -> 39.5 us
  between operations: 17.7 us -> 4.36 us
  blocking collectives: 0 us -> 7.74 us
  matrix products: 24.9 us -> 21.2 us
  other arithmetic: 12.3 us -> 10.4 us
    psum x2 -> x0, waiting for transfers between devices: 41.5 us -> none  [jacobi_step(): cross = lax.psum(inner_rows(first, second), 'row')]
    all_gather x0 -> x2, blocking collectives: none -> 7.74 us  [jacobi_step(): cross = jnp.sum(lax.all_gather(inner_rows(first, second), 'row'), axis=0)]
    reduce_sum x2, other arithmetic: 3.06 us -> 1.23 us  [couple(): coupling = cross * (2.0 / jnp.sqrt(jnp.sum(cross * cross) + 1e-06))]
    dot_general x2, matrix products: 2.37 us -> 0.54 us  [couple(): left = (identity + jnp.dot(coupling, coupling.T, precision=precise)) / 5.0]
    dot_general x2, matrix products: 2.4 us -> 0.57 us  [couple(): right = (identity + jnp.dot(coupling.T, coupling, precision=precise)) / 5.0]
  transfers between devices with their start and end apart: 6 -> 4, of which waited for: 6 -> 3; matrix products, arithmetic and copies ran while one was open for 2% -> 4% of each run, Pallas kernels for 0% -> 0%
where the time goes in v1:
time: 99.5 us; the launch traced here: 98.3 us
  waiting for transfers between devices  39.5 us (40%)
  matrix products  21.2 us (21%)
  starting transfers between devices  13.3 us (13%)
  other arithmetic  10.4 us (10%)
  blocking collectives  7.74 us (8%)
  between operations  4.36 us (4%)
  local copies, waits for them, and re-layouts  1.82 us (2%)
    ppermute x4, waiting for transfers between devices, passed_along(): lax.ppermute(value, axis, [(source, source + steps) for source in range(i...  39.5 us
    ppermute x4, starting transfers between devices, passed_along(): lax.ppermute(value, axis, [(source, source + steps) for source in range(i...  13.3 us
    all_gather x2, blocking collectives, jacobi_step(): cross = jnp.sum(lax.all_gather(inner_rows(first, second), 'row'), axis=0)  7.74 us
    dot_general x2, matrix products, inner_rows(): lax.dot_general(first, second, (((0,), (0,)), ((), ())), precision=precise)  3.63 us
    select_n x2, other arithmetic, jacobi_step(): first = jnp.where(order_flag, upper, lower)  3.4 us
    dot_general x2, matrix products, jacobi_step(): jnp.dot(second - jnp.dot(first, coupling, precision=precise), right_inver...  3.28 us
    dot_general x2, matrix products, jacobi_step(): jnp.dot(first, coupling, precision=precise)  2.93 us
    reduce_sum x1, other arithmetic, jacobi_step(): upper_id = jnp.sum(jnp.where(matching, upper_ids, 0))  2.65 us
  transfers between devices with their start and end apart: 4, of which 3 were waited for; matrix products, arithmetic and copies ran while one was open for 4% of the time, Pallas kernels for 0%

profile of v1, /device:TPU:9, one launch (start us, length us, event | category | flops | bytes accessed | tf_op | source)
XLA Modules:
  0.0 98.3 jit_solution(14807327015197611483)
XLA Ops:
  0.0 1.5 %select_reduce_fusion = (s32[]{:T(128)}, s32[]{:T(128)}) fusion(s32[32]{0:T(128)} %param.3, s32[]{:T(128)S(6)} %axis_index.12), kind=kLoop, calls=%fused_computation.82 | loop fusion | flops 78 | bytes 140 | tf_op jit(solution)/shard_map/reduce_sum | solution.py:49
  2.9 1.7 %slice_select_fusion.1 = (f32[2048,128]{1,0:T(8,128)S(1)}, f32[2048,128]{1,0:T(8,128)S(1)}) fusion(f32[2048,256]{1,0:T(8,128)} %param.2, pred[]{:T(512)S(6)} %lt.7), kind=kLoop, calls=%fused_computation.42 | loop fusion | flops 524288 | bytes 4194305 | tf_op jit(solution)/shard_map/jit(_where)/select_n | solution.py:51
  4.5 1.8 %fusion.39 = f32[128,128]{1,0:T(8,128)S(1)} fusion(f32[2048,128]{1,0:T(8,128)S(1)} %get-tuple-element.15, f32[2048,128]{1,0:T(8,128)S(1)} %get-tuple-element.16), kind=kOutput, calls=%fused_computation.86 | convolution fusion | flops 402653184 | bytes 2162688 | tf_op jit(solution)/shard_map/dot_general | solution.py:37
  6.4 3.8 %all-gather = f32[256,128]{1,0:T(8,128)S(1)} all-gather(f32[128,128]{1,0:T(8,128)S(1)} %fusion.39), channel_id=2, replica_groups=mesh['row'=2,'pair'=16] {'row'}, dimensions={0}, use_global_device_ids=true | all-gather | bytes 196608 | tf_op jit(solution)/shard_map/all_gather | solution.py:53
  10.2 0.6 multiply_reduce_fusion.1
  11.5 0.3 fusion.11
  13.0 0.3 fusion.15
  14.5 1.9 %convolution_subtract_fusion.1 = f32[2048,128]{1,0:T(8,128)} fusion(f32[2048,128]{1,0:T(8,128)S(1)} %get-tuple-element.16, f32[2048,128]{1,0:T(8,128)S(1)} %get-tuple-element.15, f32[128,128]{1,0:T(8,128)S(1)} %reduce_sum.76, f32[]{:T(128)S(6)} %div.30), kind=kOutput, calls=%fused_computation.2 | convolution fusion | flops 402931712 | bytes 3211268 | tf_op jit(solution)/shard_map/dot_general | solution.py:61
  16.4 1.0 %convolution_add_fusion.1 = f32[2048,128]{1,0:T(8,128)S(1)} fusion(f32[2048,128]{1,0:T(8,128)S(1)} %get-tuple-element.15, f32[2048,128]{1,0:T(8,128)S(1)} %get-tuple-element.16, f32[128,128]{1,0:T(8,128)S(1)} %reduce_sum.76, f32[]{:T(128)S(6)} %div.30), kind=kOutput, calls=%fused_computation.3 | convolution fusion | flops 402931712 | bytes 3211268 | tf_op jit(solution)/shard_map/dot_general | solution.py:58
  18.3 1.0 fusion.43
  19.3 2.3 %broadcast_select_fusion.11 = (f32[2048,128]{1,0:T(8,128)}, f32[2048,128]{1,0:T(8,128)}, f32[2048,128]{1,0:T(8,128)S(1)}) fusion(pred[]{:T(512)S(6)} %eq.72, f32[2048,128]{1,0:T(8,128)S(1)} %fusion.43, pred[]{:T(512)S(6)} %lt.7, f32[2048,128]{1,0:T(8,128)S(1)} %copy-done, f32[128,128]{1,0:T(8,128)S(1)} %convolution_multiply_fusion.8), kind=kOutput, calls=%fused_computation.54 | convolution fusion | flops 403439616 | bytes 5308418 | tf_op jit(solution)/shard_map/dot_general | solution.py:60
  21.6 4.8 %collective-permute-start = (f32[2048,128]{1,0:T(8,128)}, f32[2048,128]{1,0:T(8,128)S(1)}, u32[]{:S(2)}, u32[]{:S(2)}) collective-permute-start(f32[2048,128]{1,0:T(8,128)} %get-tuple-element.10), channel_id=1, source_target_pairs={{0,1},{1,2},{2,3},{3,4},{4,5},{5,6},{6,7},{7,8},{8,9},{9,10},{10,1... | collective-permute-start | bytes 3145736 | tf_op jit(solution)/shard_map/ppermute | solution.py:14
  26.4 1.9 %collective-permute-start.1 = (f32[2048,128]{1,0:T(8,128)}, f32[2048,128]{1,0:T(8,128)S(1)}, u32[]{:S(2)}, u32[]{:S(2)}) collective-permute-start(f32[2048,128]{1,0:T(8,128)} %get-tuple-element.11), channel_id=1, source_target_pairs={{1,0},{2,1},{3,2},{4,3},{5,4},{6,5},{7,6},{8,7},{9,8},{10,9},{11,1... | collective-permute-start | bytes 3145736 | tf_op jit(solution)/shard_map/ppermute | solution.py:14
  28.5 0.7 fusion.38
  29.2 2.6 %fusion.36 = (s32[]{:T(128)}, s32[]{:T(128)}) fusion(s32[14]{0:T(128)S(1)} %slice.34, s32[1]{0:T(128)} %get-tuple-element.20, s32[1]{0:T(128)} %get-tuple-element.21, s32[]{:T(128)S(6)} %axis_index.12, s32[1]{0:T(128)} %get-tuple-element.19, s32[15]{0:T(128)S(1)} %slice.35), kind=kLoop, calls=%fused_computation.79 | loop fusion | flops 126 | bytes 140 | tf_op jit(solution)/shard_map/reduce_sum | solution.py:48
  33.0 16.7 %collective-permute-done = f32[2048,128]{1,0:T(8,128)S(1)} collective-permute-done((f32[2048,128]{1,0:T(8,128)}, f32[2048,128]{1,0:T(8,128)S(1)}, u32[]{:S(2)}, u32[]{:S(2)}) %collective-permute-start) | collective-permute-done | bytes 1048608 | tf_op jit(solution)/shard_map/ppermute | solution.py:14
  49.7 1.8 %collective-permute-done.1 = f32[2048,128]{1,0:T(8,128)S(1)} collective-permute-done((f32[2048,128]{1,0:T(8,128)}, f32[2048,128]{1,0:T(8,128)S(1)}, u32[]{:S(2)}, u32[]{:S(2)}) %collective-permute-start.1) | collective-permute-done | bytes 1048608 | tf_op jit(solution)/shard_map/ppermute | solution.py:14
  51.5 1.0 %copy-done.2 = f32[2048,128]{1,0:T(8,128)} copy-done((f32[2048,128]{1,0:T(8,128)}, f32[2048,128]{1,0:T(8,128)S(1)}, u32[]{:S(2)}) %copy-start.2) | copy-done | bytes 1048600
  52.5 1.7 %broadcast_select_fusion.7 = (f32[2048,128]{1,0:T(8,128)S(1)}, f32[2048,128]{1,0:T(8,128)S(1)}) fusion(pred[]{:T(512)S(6)} %lt.6, f32[2048,128]{1,0:T(8,128)S(1)} %get-tuple-element.12, f32[2048,128]{1,0:T(8,128)} %copy-done.1, pred[]{:T(512)S(6)} %eq.72, f32[2048,128]{1,0:T(8,128)} %copy-done.2, pred[]{:T(512)S(6)} %eq.76), kind=kLoop, calls=%fused_computation.50 | loop fusion | flops 1048576 | bytes 5242883 | tf_op jit(solution)/shard_map/jit(_where)/select_n | solution.py:51
  54.2 1.8 %fusion.47 = f32[128,128]{1,0:T(8,128)S(1)} fusion(f32[2048,128]{1,0:T(8,128)S(1)} %get-tuple-element.13, f32[2048,128]{1,0:T(8,128)S(1)} %get-tuple-element.14), kind=kOutput, calls=%fused_computation.94 | convolution fusion | flops 402653184 | bytes 2162688 | tf_op jit(solution)/shard_map/dot_general | solution.py:37
  56.0 4.0 %all-gather.1 = f32[256,128]{1,0:T(8,128)S(1)} all-gather(f32[128,128]{1,0:T(8,128)S(1)} %fusion.47), channel_id=3, replica_groups=mesh['row'=2,'pair'=16] {'row'}, dimensions={0}, use_global_device_ids=true | all-gather | bytes 196608 | tf_op jit(solution)/shard_map/all_gather | solution.py:53
  60.0 0.6 multiply_reduce_fusion
  61.3 0.3 fusion.3
  62.8 0.3 fusion.7
  64.3 1.0 %convolution_subtract_fusion = f32[2048,128]{1,0:T(8,128)S(1)} fusion(f32[2048,128]{1,0:T(8,128)S(1)} %get-tuple-element.14, f32[2048,128]{1,0:T(8,128)S(1)} %get-tuple-element.13, f32[128,128]{1,0:T(8,128)S(1)} %reduce_sum.78, f32[]{:T(128)S(6)} %div.35), kind=kOutput, calls=%fused_computation | convolution fusion | flops 402931712 | bytes 3211268 | tf_op jit(solution)/shard_map/dot_general | solution.py:61
  65.3 1.0 %convolution_add_fusion = f32[2048,128]{1,0:T(8,128)S(1)} fusion(f32[2048,128]{1,0:T(8,128)S(1)} %get-tuple-element.13, f32[2048,128]{1,0:T(8,128)S(1)} %get-tuple-element.14, f32[128,128]{1,0:T(8,128)S(1)} %reduce_sum.78, f32[]{:T(128)S(6)} %div.35), kind=kOutput, calls=%fused_computation.1 | convolution fusion | flops 402931712 | bytes 3211268 | tf_op jit(solution)/shard_map/dot_general | solution.py:58
  67.1 1.0 %fusion.51 = f32[2048,128]{1,0:T(8,128)S(1)} fusion(f32[2048,128]{1,0:T(8,128)S(1)} %convolution_add_fusion, f32[128,128]{1,0:T(8,128)S(1)} %convolution_multiply_fusion.4), kind=kOutput, calls=%fused_computation.98 | convolution fusion | flops 402653184 | bytes 2162688 | tf_op jit(solution)/shard_map/dot_general | solution.py:57
  68.1 1.0 %broadcast_select_fusion.9 = (f32[2048,128]{1,0:T(8,128)S(1)}, f32[2048,128]{1,0:T(8,128)S(1)}, f32[2048,128]{1,0:T(8,128)S(1)}) fusion(pred[]{:T(512)S(6)} %eq.72, f32[2048,128]{1,0:T(8,128)S(1)} %fusion.51, pred[]{:T(512)S(6)} %lt.6, f32[2048,128]{1,0:T(8,128)S(1)} %convolution_subtract_fusion, f32[128,128]{1,0:T(8,128)S(1)} %convolution_multiply_fusion), kind=kOutput, calls=%fused_computation.52 | convolution fusion | flops 403439616 | bytes 5308418 | tf_op jit(solution)/shard_map/dot_general | solution.py:60
  69.1 4.6 %collective-permute-start.2 = (f32[2048,128]{1,0:T(8,128)S(1)}, f32[2048,128]{1,0:T(8,128)S(1)}, u32[]{:S(2)}, u32[]{:S(2)}) collective-permute-start(f32[2048,128]{1,0:T(8,128)S(1)} %get-tuple-element.7), channel_id=1, source_target_pairs={{0,1},{1,2},{2,3},{3,4},{4,5},{5,6},{6,7},{7,8},{8,9},{9,10},{10,1... | collective-permute-start | bytes 3145736 | tf_op jit(solution)/shard_map/ppermute | solution.py:14
  73.8 1.9 %collective-permute-start.3 = (f32[2048,128]{1,0:T(8,128)S(1)}, f32[2048,128]{1,0:T(8,128)S(1)}, u32[]{:S(2)}, u32[]{:S(2)}) collective-permute-start(f32[2048,128]{1,0:T(8,128)S(1)} %get-tuple-element.8), channel_id=1, source_target_pairs={{1,0},{2,1},{3,2},{4,3},{5,4},{6,5},{7,6},{8,7},{9,8},{10,9},{11,1... | collective-permute-start | bytes 3145736 | tf_op jit(solution)/shard_map/ppermute | solution.py:14
  75.7 21.0 %collective-permute-done.2 = f32[2048,128]{1,0:T(8,128)S(1)} collective-permute-done((f32[2048,128]{1,0:T(8,128)S(1)}, f32[2048,128]{1,0:T(8,128)S(1)}, u32[]{:S(2)}, u32[]{:S(2)}) %collective-permute-start.2) | collective-permute-done | bytes 1048608 | tf_op jit(solution)/shard_map/ppermute | solution.py:14
  96.9 1.5 %pad_maximum_fusion = f32[2048,256]{1,0:T(8,128)} fusion(f32[2048,128]{1,0:T(8,128)S(1)} %get-tuple-element.18, f32[2048,128]{1,0:T(8,128)S(1)} %get-tuple-element.17), kind=kLoop, calls=%fused_computation.4 | loop fusion | flops 524288 | bytes 4194304 | tf_op jit(solution)/shard_map/concatenate | solution.py:84
  (45 shorter events, 6.7 us)
Async XLA Ops:
  17.4 1.8 %copy-start = (f32[2048,128]{1,0:T(8,128)S(1)}, f32[2048,128]{1,0:T(8,128)}, u32[]{:S(2)}) copy-start(f32[2048,128]{1,0:T(8,128)} %convolution_subtract_fusion.1) | copy-start | bytes 3145732
  19.3 9.1 %copy-start.3 = (s32[32]{0:T(128)S(1)}, s32[32]{0:T(128)}, u32[]{:S(2)}) copy-start(s32[32]{0:T(128)} %param.3) | copy-start | bytes 388
  21.6 28.1 %collective-permute-start = (f32[2048,128]{1,0:T(8,128)}, f32[2048,128]{1,0:T(8,128)S(1)}, u32[]{:S(2)}, u32[]{:S(2)}) collective-permute-start(f32[2048,128]{1,0:T(8,128)} %get-tuple-element.10), channel_id=1, source_target_pairs={{0,1},{1,2},{2,3},{3,4},{4,5},{5,6},{6,7},{7,8},{8,9},{9,10},{10,1... | collective-permute-start | bytes 3145736 | tf_op jit(solution)/shard_map/ppermute | solution.py:14
  26.4 25.1 %collective-permute-start.1 = (f32[2048,128]{1,0:T(8,128)}, f32[2048,128]{1,0:T(8,128)S(1)}, u32[]{:S(2)}, u32[]{:S(2)}) collective-permute-start(f32[2048,128]{1,0:T(8,128)} %get-tuple-element.11), channel_id=1, source_target_pairs={{1,0},{2,1},{3,2},{4,3},{5,4},{6,5},{7,6},{8,7},{9,8},{10,9},{11,1... | collective-permute-start | bytes 3145736 | tf_op jit(solution)/shard_map/ppermute | solution.py:14
  49.7 1.8 %copy-start.1 = (f32[2048,128]{1,0:T(8,128)}, f32[2048,128]{1,0:T(8,128)S(1)}, u32[]{:S(2)}) copy-start(f32[2048,128]{1,0:T(8,128)S(1)} %collective-permute-done) | copy-start | bytes 3145732
  51.5 1.0 %copy-start.2 = (f32[2048,128]{1,0:T(8,128)}, f32[2048,128]{1,0:T(8,128)S(1)}, u32[]{:S(2)}) copy-start(f32[2048,128]{1,0:T(8,128)S(1)} %collective-permute-done.1) | copy-start | bytes 3145732
  69.1 27.6 %collective-permute-start.2 = (f32[2048,128]{1,0:T(8,128)S(1)}, f32[2048,128]{1,0:T(8,128)S(1)}, u32[]{:S(2)}, u32[]{:S(2)}) collective-permute-start(f32[2048,128]{1,0:T(8,128)S(1)} %get-tuple-element.7), channel_id=1, source_target_pairs={{0,1},{1,2},{2,3},{3,4},{4,5},{5,6},{6,7},{7,8},{8,9},{9,10},{10,1... | collective-permute-start | bytes 3145736 | tf_op jit(solution)/shard_map/ppermute | solution.py:14
  73.8 23.0 %collective-permute-start.3 = (f32[2048,128]{1,0:T(8,128)S(1)}, f32[2048,128]{1,0:T(8,128)S(1)}, u32[]{:S(2)}, u32[]{:S(2)}) collective-permute-start(f32[2048,128]{1,0:T(8,128)S(1)} %get-tuple-element.8), channel_id=1, source_target_pairs={{1,0},{2,1},{3,2},{4,3},{5,4},{6,5},{7,6},{8,7},{9,8},{10,9},{11,1... | collective-permute-start | bytes 3145736 | tf_op jit(solution)/shard_map/ppermute | solution.py:14
